TPU v7x, 512 devices: a whole 4x4x16 slice. The times are simulated.
512 devices in a mesh: group: 16 (over z), shard: 32 (over y, x, core).
Axes of the slice: x: 4, y: 4, z: 16, core: 2. Of those that a mesh axis runs over, the one named last changes fastest.
Arguments:
- entry_grads: float32 [16, 32, 256, 1280], P('group', 'shard'), may hold values from -800 to 800
- exit_grads: float32 [16, 32, 256, 1024], P('group', 'shard'), may hold values from -800 to 800
- entry_params: float32 [32, 256, 1280], P('shard', 'group'), may hold values from -0.15625 to 0.15625
- exit_params: float32 [32, 256, 1024], P('shard', 'group'), may hold values from -0.15625 to 0.15625
- entry_mean: float32 [32, 256, 1280], P('shard', 'group'), may hold values from -1.5 to 1.5
- exit_mean: float32 [32, 256, 1024], P('shard', 'group'), may hold values from -1.5 to 1.5
- entry_square: float32 [32, 256, 1280], P('shard', 'group'), may hold values from 0.01 to 1
- exit_square: float32 [32, 256, 1024], P('shard', 'group'), may hold values from 0.01 to 1
Outputs:
- entry_master: float32 [32, 256, 1280], P('shard', 'group')
- exit_master: float32 [32, 256, 1024], P('shard', 'group')
- entry_moment: float32 [32, 256, 1280], P('shard', 'group')
- exit_moment: float32 [32, 256, 1024], P('shard', 'group')
- entry_variance: float32 [32, 256, 1280], P('shard', 'group')
- exit_variance: float32 [32, 256, 1024], P('shard', 'group')
- entry_weights: bfloat16 [32, 256, 1280], P('shard')
- exit_weights: bfloat16 [32, 256, 1024], P('shard')
All inputs are finite; a program needn't handle non-finite values.
Results may differ from a plain program's by a relative error of at most 0.0004.
Values may be sent and summed in bfloat16 or wider, within the bound.
No kernel may reach another device: no remote copies, remote signals or barrier semaphores. Data moves between devices by JAX's collectives and lax.ppermute only.
A program may use at most 64 MiB of HBM per device.

v0:
```python
import jax
import jax.numpy as jnp
from jax import lax
from jax.sharding import PartitionSpec as P

beta_first = 0.9
beta_second = 0.95
learn_rate = 0.01
decay_rate = 0.1
epsilon = 1e-08
correct_first = 1.0 - 0.9**40
correct_second = 1.0 - 0.95**40


def adamw_step(params, mean, square, total, clip):
    grads = clip * total
    moment = beta_first * mean + (1.0 - beta_first) * grads
    variance = beta_second * square + (1.0 - beta_second) * grads * grads
    update = moment / correct_first / (jnp.sqrt(variance / correct_second) + epsilon)
    master = params - learn_rate * (update + decay_rate * params)
    return (master, moment, variance)


def sum_everywhere(values):
    axes = ("group", "shard")
    lanes = jnp.sum(values.reshape(-1, 128), axis=0)
    sent = jnp.broadcast_to(lanes, (lax.axis_size(axes), 1, 128))
    return jnp.sum(lax.all_to_all(sent, axes, 0, 0))


def body(
    entry_grads,
    exit_grads,
    entry_params,
    exit_params,
    entry_mean,
    exit_mean,
    entry_square,
    exit_square,
):
    entry_rows_dev = entry_grads.shape[2]
    exit_rows_dev = exit_grads.shape[2]
    entry_width = entry_grads.shape[3]
    exit_width = exit_grads.shape[3]
    entry_local = entry_grads.reshape(entry_rows_dev, entry_width)
    exit_local = exit_grads.reshape(exit_rows_dev, exit_width)
    packed = jnp.concatenate([entry_local, exit_local], axis=1)
    total = lax.psum_scatter(packed, "group", scatter_dimension=0, tiled=True)
    entry_total = total[:, :entry_width]
    exit_total = total[:, entry_width:]
    squares = sum_everywhere(total * total)
    count = (entry_rows_dev * entry_width + exit_rows_dev * exit_width) * lax.axis_size("shard")
    limit = jnp.sqrt(jnp.float32(count))
    clip = jnp.minimum(jnp.float32(1.0), limit / (jnp.sqrt(squares) + 1e-06))
    entry_master, entry_moment, entry_variance = adamw_step(
        entry_params[0], entry_mean[0], entry_square[0], entry_total, clip
    )
    exit_master, exit_moment, exit_variance = adamw_step(
        exit_params[0], exit_mean[0], exit_square[0], exit_total, clip
    )
    entry_round = entry_master.astype(jnp.bfloat16)
    exit_round = exit_master.astype(jnp.bfloat16)
    entry_weights = lax.all_gather(entry_round, "group", axis=0, tiled=True)
    exit_weights = lax.all_gather(exit_round, "group", axis=0, tiled=True)
    return (
        entry_master[None],
        exit_master[None],
        entry_moment[None],
        exit_moment[None],
        entry_variance[None],
        exit_variance[None],
        entry_weights[None],
        exit_weights[None],
    )


def solution(mesh):
    placed = (
        P("group", "shard", None, None),
        P("group", "shard", None, None),
        P("shard", "group", None),
        P("shard", "group", None),
        P("shard", "group", None),
        P("shard", "group", None),
        P("shard", "group", None),
        P("shard", "group", None),
    )
    return jax.shard_map(
        body,
        mesh=mesh,
        in_specs=placed,
        out_specs=(
            P("shard", "group", None),
            P("shard", "group", None),
            P("shard", "group", None),
            P("shard", "group", None),
            P("shard", "group", None),
            P("shard", "group", None),
            P("shard", None, None),
            P("shard", None, None),
        ),
        check_vma=False,
    )
```

profile of v0, /device:TPU:2, one launch (start us, length us, event | category | flops | bytes accessed | tf_op | source)
XLA Modules:
  0.0 204.4 jit_solution(7940237761173604504)
XLA Ops:
  7.2 0.0 reduce-scatter.2.cloned.1.call-start
  7.2 3.2 %pad_maximum_fusion = f32[256,2304]{1,0:T(8,128)} fusion(f32[256,1024]{1,0:T(8,128)} %bitcast.67, f32[256,1280]{1,0:T(8,128)} %bitcast.65), kind=kLoop, calls=%fused_computation | loop fusion | flops 589824 | bytes 4718592 | tf_op jit(solution)/shard_map/concatenate | solution.py:47
  10.4 0.0 copy-start.4
  10.4 0.0 copy-start.5
  10.4 0.0 copy-start.6
  10.4 0.0 copy-start.1
  10.4 0.0 copy-start.2
  10.5 0.0 copy-start.3
  10.5 0.0 reduce-scatter.2.cloned.1.call-update
  10.5 78.5 %reduce-scatter.2.cloned.1.call-done = f32[16,2304]{1,0:T(8,128)} async-done(((f32[256,2304]{1,0:T(8,128)}), f32[16,2304]{1,0:T(8,128)}) %reduce-scatter.2.cloned.1.call-update) | async-done | bytes 147472 | tf_op jit(solution)/shard_map/reduce_scatter | solution.py:48
  89.0 0.0 copy-start
  89.0 1.1 mul.96
  90.1 0.1 reduce_sum.18
  90.2 0.1 broadcast_in_dim.27
  90.3 40.8 %all_to_all.5 = f32[512,1,128]{2,1,0:T(1,128)S(1)} all-to-all(f32[512,1,128]{2,1,0:T(1,128)S(1)} %broadcast_in_dim.27), channel_id=1, replica_groups=mesh['group'=16,'shard'=32] {'group','shard'}, dimensions={0} | all-to-all | bytes 524288 | tf_op jit(solution)/shard_map/all_to_all | solution.py:28
  131.1 0.7 reduce_sum.19
  132.5 0.0 copy-done.4
  132.5 0.0 copy-done.5
  132.5 0.0 copy-done.6
  132.5 1.5 fusion.10
  134.1 30.4 %all_gather.7 = bf16[256,1024]{1,0:T(8,128)(2,1)S(1)} all-gather(bf16[16,1024]{1,0:T(8,128)(2,1)S(1)} %get-tuple-element.8), channel_id=1, replica_groups=mesh['group'=16,'shard'=32] {'group'}, dimensions={0}, use_global_device_ids=true | all-gather | bytes 557056 | tf_op jit(solution)/shard_map/all_gather | solution.py:64
  164.5 0.0 copy-done.1
  164.5 0.0 copy-done.2
  164.5 0.0 copy-done.3
  164.5 0.0 copy-done
  164.5 0.7 fusion.11
  165.2 30.7 %all_gather.6 = bf16[256,1280]{1,0:T(8,128)(2,1)S(1)} all-gather(bf16[16,1280]{1,0:T(8,128)(2,1)S(1)} %get-tuple-element.10), channel_id=1, replica_groups=mesh['group'=16,'shard'=32] {'group'}, dimensions={0}, use_global_device_ids=true | all-gather | bytes 696320 | tf_op jit(solution)/shard_map/all_gather | solution.py:63
  195.9 0.8 copy.19
  196.8 0.8 copy.20
  (1 shorter events, 0.0 us)
Async XLA Ops:
  7.2 81.9 %reduce-scatter.2.cloned.1.call-start = ((), (), s32[]{:S(2)}) async-start(), calls=%async_computation.2 | async-start | bytes 2506752 | tf_op jit(solution)/shard_map/reduce_scatter | solution.py:48
  10.4 122.1 %copy-start.4 = (f32[1,16,1024]{2,1,0:T(8,128)S(1)}, f32[1,16,1024]{2,1,0:T(8,128)}, u32[]{:S(2)}) copy-start(f32[1,16,1024]{2,1,0:T(8,128)} %param.15) | copy-start | bytes 196612
  10.4 122.1 %copy-start.5 = (f32[1,16,1024]{2,1,0:T(8,128)S(1)}, f32[1,16,1024]{2,1,0:T(8,128)}, u32[]{:S(2)}) copy-start(f32[1,16,1024]{2,1,0:T(8,128)} %param.13) | copy-start | bytes 196612
  10.4 122.1 %copy-start.6 = (f32[1,16,1024]{2,1,0:T(8,128)S(1)}, f32[1,16,1024]{2,1,0:T(8,128)}, u32[]{:S(2)}) copy-start(f32[1,16,1024]{2,1,0:T(8,128)} %param.11) | copy-start | bytes 196612
  10.4 154.1 %copy-start.1 = (f32[1,16,1280]{2,1,0:T(8,128)S(1)}, f32[1,16,1280]{2,1,0:T(8,128)}, u32[]{:S(2)}) copy-start(f32[1,16,1280]{2,1,0:T(8,128)} %param.14) | copy-start | bytes 245764
  10.4 154.1 %copy-start.2 = (f32[1,16,1280]{2,1,0:T(8,128)S(1)}, f32[1,16,1280]{2,1,0:T(8,128)}, u32[]{:S(2)}) copy-start(f32[1,16,1280]{2,1,0:T(8,128)} %param.12) | copy-start | bytes 245764
  10.5 154.1 %copy-start.3 = (f32[1,16,1280]{2,1,0:T(8,128)S(1)}, f32[1,16,1280]{2,1,0:T(8,128)}, u32[]{:S(2)}) copy-start(f32[1,16,1280]{2,1,0:T(8,128)} %param.10) | copy-start | bytes 245764
  89.0 75.5 %copy-start = (f32[16,2304]{1,0:T(8,128)S(1)}, f32[16,2304]{1,0:T(8,128)}, u32[]{:S(2)}) copy-start(f32[16,2304]{1,0:T(8,128)} %reduce-scatter.2.cloned.1.call-done) | copy-start | bytes 442372
Sparse Core Ops, SparseCore 0:
  10.8 78.1 reduce-scatter.1
where the time goes:
time: 205 us; the launch traced here: 204 us
  blocking collectives  102 us (50%)
  waiting for transfers between devices  78.6 us (38%)
  between operations  14.8 us (7%)
  other arithmetic  7.27 us (4%)
    reduce_scatter x1, waiting for transfers between devices, body(): total = lax.psum_scatter(packed, 'group', scatter_dimension=0, tiled=True)  78.5 us
    all_to_all x1, blocking collectives, sum_everywhere(): return jnp.sum(lax.all_to_all(sent, axes, 0, 0))  40.8 us
    all_gather x1, blocking collectives, body(): entry_weights = lax.all_gather(entry_round, 'group', axis=0, tiled=True)  30.7 us
    all_gather x1, blocking collectives, body(): exit_weights = lax.all_gather(exit_round, 'group', axis=0, tiled=True)  30.4 us
  transfers between devices with their start and end apart: 1, of which 1 were waited for; matrix products, arithmetic and copies ran while one was open for 0% of the time, Pallas kernels for 0%

commit v1 on v0

--- a/solution.py
+++ b/solution.py
@@ -60,8 +60,13 @@
     )
     entry_round = entry_master.astype(jnp.bfloat16)
     exit_round = exit_master.astype(jnp.bfloat16)
-    entry_weights = lax.all_gather(entry_round, "group", axis=0, tiled=True)
-    exit_weights = lax.all_gather(exit_round, "group", axis=0, tiled=True)
+    entry_weights, exit_weights = jnp.split(
+        lax.all_gather(
+            jnp.concatenate([entry_round, exit_round], axis=1), "group", axis=0, tiled=True
+        ),
+        [entry_round.shape[1]],
+        axis=1,
+    )
     return (
         entry_master[None],
         exit_master[None],

time: 205 us -> 207 us (level)
  waiting for transfers between devices: 78.6 us -> 140 us
  blocking collectives: 102 us -> 40.8 us
  local copies, waits for them, and re-layouts: 1.81 us -> 4.02 us
    all_gather x0 -> x1, waiting for transfers between devices: none -> 61.2 us  [body(): lax.all_gather(jnp.concatenate([entry_round, exit_round], axis=1), 'group...]
    all_gather x2 -> x0, blocking collectives: 61.1 us -> none  [the longest x1 30.7 us: body(): entry_weights = lax.all_gather(entry_round, 'group', axis=0, tiled=True)]
    broadcast_in_dim x0 -> x2, local copies, waits for them, and re-layouts: none -> 3.83 us  [the longest x1 1.96 us: body(): entry_weights[None]]
  transfers between devices with their start and end apart: 1 -> 2, of which waited for: 1 -> 2; matrix products, arithmetic and copies ran while one was open for 0% -> 0% of each run, Pallas kernels for 0% -> 0%
where the time goes in v1:
time: 207 us
  waiting for transfers between devices  140 us (68%)
  blocking collectives  40.8 us (20%)
  between operations  14.9 us (7%)
  other arithmetic  7.05 us (3%)
  local copies, waits for them, and re-layouts  4.02 us (2%)
    reduce_scatter x1, waiting for transfers between devices, body(): total = lax.psum_scatter(packed, 'group', scatter_dimension=0, tiled=True)  78.5 us
    all_gather x1, waiting for transfers between devices, body(): lax.all_gather(jnp.concatenate([entry_round, exit_round], axis=1), 'group...  61.2 us
    all_to_all x1, blocking collectives, sum_everywhere(): return jnp.sum(lax.all_to_all(sent, axes, 0, 0))  40.8 us
  transfers between devices with their start and end apart: 2, of which 2 were waited for; matrix products, arithmetic and copies ran while one was open for 0% of the time, Pallas kernels for 0%

profile of v1, /device:TPU:2, one launch (start us, length us, event | category | flops | bytes accessed | tf_op | source)
XLA Modules:
  0.0 206.5 jit_solution(15535089711261778054)
XLA Ops:
  7.2 0.0 reduce-scatter.2.cloned.1.call-start
  7.2 3.2 %pad_maximum_fusion = f32[256,2304]{1,0:T(8,128)} fusion(f32[256,1024]{1,0:T(8,128)} %bitcast.67, f32[256,1280]{1,0:T(8,128)} %bitcast.65), kind=kLoop, calls=%fused_computation | loop fusion | flops 589824 | bytes 4718592 | tf_op jit(solution)/shard_map/concatenate | solution.py:47
  10.4 0.0 reduce-scatter.2.cloned.1.call-update
  10.4 0.0 copy-start.4
  10.4 0.0 copy-start.5
  10.5 0.0 copy-start.6
  10.5 0.0 copy-start.1
  10.5 0.0 copy-start.2
  10.5 0.0 copy-start.3
  10.5 0.0 all-gather.2.cloned.1.call-start
  10.6 78.5 %reduce-scatter.2.cloned.1.call-done = f32[16,2304]{1,0:T(8,128)} async-done(((f32[256,2304]{1,0:T(8,128)}), f32[16,2304]{1,0:T(8,128)}) %reduce-scatter.2.cloned.1.call-update) | async-done | bytes 147472 | tf_op jit(solution)/shard_map/reduce_scatter | solution.py:48
  89.0 0.0 copy-start
  89.0 1.1 mul.96
  90.1 0.1 reduce_sum.18
  90.2 0.1 broadcast_in_dim.27
  90.3 40.8 %all_to_all.5 = f32[512,1,128]{2,1,0:T(1,128)S(1)} all-to-all(f32[512,1,128]{2,1,0:T(1,128)S(1)} %broadcast_in_dim.27), channel_id=1, replica_groups=mesh['group'=16,'shard'=32] {'group','shard'}, dimensions={0} | all-to-all | bytes 524288 | tf_op jit(solution)/shard_map/all_to_all | solution.py:28
  131.1 0.7 reduce_sum.19
  132.5 0.0 copy-done.4
  132.5 0.0 copy-done.5
  132.5 0.0 copy-done.6
  132.5 0.0 copy-done
  132.6 0.7 fusion.11
  133.3 0.0 copy-done.1
  133.3 0.0 copy-done.2
  133.3 0.0 copy-done.3
  133.3 0.7 fusion.10
  134.0 0.6 pad_maximum_fusion.1
  134.6 0.0 all-gather.2.cloned.1.call-update
  134.7 61.2 %all-gather.2.cloned.1.call-done = bf16[256,2304]{1,0:T(8,128)(2,1)} async-done(((bf16[16,2304]{1,0:T(8,128)(2,1)}), bf16[256,2304]{1,0:T(8,128)(2,1)}) %all-gather.2.cloned.1.call-update) | async-done | bytes 1179664 | tf_op jit(solution)/shard_map/all_gather | solution.py:64
  195.8 1.9 slice_bitcast_fusion.1
  197.7 2.0 slice_bitcast_fusion
  (1 shorter events, 0.0 us)
Async XLA Ops:
  7.2 81.9 %reduce-scatter.2.cloned.1.call-start = ((), (), s32[]{:S(2)}) async-start(), calls=%async_computation.2 | async-start | bytes 2506752 | tf_op jit(solution)/shard_map/reduce_scatter | solution.py:48
  10.4 122.1 %copy-start.4 = (f32[1,16,1024]{2,1,0:T(8,128)S(1)}, f32[1,16,1024]{2,1,0:T(8,128)}, u32[]{:S(2)}) copy-start(f32[1,16,1024]{2,1,0:T(8,128)} %param.15) | copy-start | bytes 196612
  10.4 122.1 %copy-start.5 = (f32[1,16,1024]{2,1,0:T(8,128)S(1)}, f32[1,16,1024]{2,1,0:T(8,128)}, u32[]{:S(2)}) copy-start(f32[1,16,1024]{2,1,0:T(8,128)} %param.13) | copy-start | bytes 196612
  10.5 122.1 %copy-start.6 = (f32[1,16,1024]{2,1,0:T(8,128)S(1)}, f32[1,16,1024]{2,1,0:T(8,128)}, u32[]{:S(2)}) copy-start(f32[1,16,1024]{2,1,0:T(8,128)} %param.11) | copy-start | bytes 196612
  10.5 122.8 %copy-start.1 = (f32[1,16,1280]{2,1,0:T(8,128)S(1)}, f32[1,16,1280]{2,1,0:T(8,128)}, u32[]{:S(2)}) copy-start(f32[1,16,1280]{2,1,0:T(8,128)} %param.14) | copy-start | bytes 245764
  10.5 122.8 %copy-start.2 = (f32[1,16,1280]{2,1,0:T(8,128)S(1)}, f32[1,16,1280]{2,1,0:T(8,128)}, u32[]{:S(2)}) copy-start(f32[1,16,1280]{2,1,0:T(8,128)} %param.12) | copy-start | bytes 245764
  10.5 122.8 %copy-start.3 = (f32[1,16,1280]{2,1,0:T(8,128)S(1)}, f32[1,16,1280]{2,1,0:T(8,128)}, u32[]{:S(2)}) copy-start(f32[1,16,1280]{2,1,0:T(8,128)} %param.10) | copy-start | bytes 245764
  10.5 185.3 %all-gather.2.cloned.1.call-start = ((), (), s32[]{:S(2)}) async-start(), calls=%async_computation.3 | async-start | bytes 1253376 | tf_op jit(solution)/shard_map/all_gather | solution.py:64
  89.0 43.5 %copy-start = (f32[16,2304]{1,0:T(8,128)S(1)}, f32[16,2304]{1,0:T(8,128)}, u32[]{:S(2)}) copy-start(f32[16,2304]{1,0:T(8,128)} %reduce-scatter.2.cloned.1.call-done) | copy-start | bytes 442372
Sparse Core Ops, SparseCore 0:
  10.8 78.1 reduce-scatter.1
  134.8 61.0 all-gather.1
